TPU v7x, 32 devices: a whole 2x2x4 slice. The times are simulated.
32 devices in a mesh: dp: 2 (over x), tm: 4 (over y, core), height: 4 (over z).
Axes of the slice: x: 2, y: 2, z: 4, core: 2. Of those that a mesh axis runs over, the one named last changes fastest.
Arguments:
- frames_in: bfloat16 [2, 12, 12, 320, 128], P('dp', 'tm', 'height'), may hold values from -6 to 6
- grad_out: bfloat16 [2, 12, 12, 320, 128], P('dp', 'tm', 'height'), may hold values from -6 to 6
- w_spatial: bfloat16 [3, 3, 128, 128], replicated, may hold values from -0.1875 to 0.1875
- w_temporal: bfloat16 [3, 128, 128], replicated, may hold values from -0.3125 to 0.3125
Outputs:
- layer_out: bfloat16 [2, 12, 12, 320, 128], P('dp', 'tm', 'height')
- grad_in: bfloat16 [2, 12, 12, 320, 128], P('dp', 'tm', 'height')
- grad_spatial: float32 [3, 3, 128, 128], replicated
- grad_temporal: float32 [3, 128, 128], replicated
All inputs are finite; a program needn't handle non-finite values.
Results may differ from a plain program's by a relative error of at most 0.005.
Values may be sent and summed in bfloat16 or wider, within the bound.
A program may use at most 64 MiB of HBM per device.

v0:
```python
import math

import jax
import jax.numpy as jnp
from jax import lax
from jax.sharding import PartitionSpec as P


def extended(value, sides, width):
    for axis, dim in sides:
        count, length = (lax.axis_size(axis), value.shape[dim])
        up = [(i, (i + 1) % count) for i in range(count - 1)]
        down = [(j, i) for i, j in up]
        last = lax.slice_in_dim(value, length - width, length, axis=dim)
        leading = lax.slice_in_dim(value, 0, width, axis=dim)
        before = lax.ppermute(last, axis, up)
        after = lax.ppermute(leading, axis, down)
        value = jnp.concatenate([before, value, after], axis=dim)
    return value


def shifted(value, axis, by):
    count = lax.axis_size(axis)
    pairs = [(i, i + by) for i in range(count) if 0 <= i + by < count]
    return lax.ppermute(value, axis, pairs)


def column_stack(source):
    width_len = source.shape[3]
    padded = jnp.pad(source, ((0, 0), (0, 0), (0, 0), (1, 1), (0, 0)))
    return jnp.concatenate(
        [padded[:, :, :, col_tap : col_tap + width_len] for col_tap in range(3)], axis=4
    )


def spatial_conv(stacked, w_spatial, row_count):
    channels = w_spatial.shape[3]
    summed = None
    for row_tap in range(3):
        matrix = w_spatial[row_tap].reshape(3 * channels, channels)
        partial_value = jnp.einsum(
            "bfrwk,kd->bfrwd",
            stacked[:, :, row_tap : row_tap + row_count],
            matrix,
            preferred_element_type=jnp.float32,
        )
        summed = partial_value if summed is None else summed + partial_value
    return summed


def per_device(frames_in, grad_out, w_spatial, w_temporal):
    clip_count, frame_count, row_count, col_count, channels = frames_in.shape
    with_rows = extended(frames_in, (("height", 2),), 1)
    stacked = column_stack(with_rows)
    pre_act = spatial_conv(stacked, w_spatial, row_count)
    hidden = jax.nn.silu(pre_act).astype(jnp.bfloat16)
    earlier = shifted(hidden[:, frame_count - 2 :], "tm", 1)
    hidden_ext = jnp.concatenate([earlier, hidden], axis=1)
    mixed = None
    for lag_tap in range(3):
        partial_value = jnp.einsum(
            "bfrwc,cd->bfrwd",
            hidden_ext[:, 2 - lag_tap : 2 - lag_tap + frame_count],
            w_temporal[lag_tap],
            preferred_element_type=jnp.float32,
        )
        mixed = partial_value if mixed is None else mixed + partial_value
    layer_out = mixed.astype(jnp.bfloat16)
    later = shifted(grad_out[:, :2], "tm", -1)
    grad_ext = jnp.concatenate([grad_out, later], axis=1)
    grad_hidden = None
    for lag_tap in range(3):
        partial_value = jnp.einsum(
            "bfrwd,cd->bfrwc",
            grad_ext[:, lag_tap : lag_tap + frame_count],
            w_temporal[lag_tap],
            preferred_element_type=jnp.float32,
        )
        grad_hidden = partial_value if grad_hidden is None else grad_hidden + partial_value
    temporal_local = jnp.stack(
        [
            jnp.einsum(
                "bfrwc,bfrwd->cd",
                hidden_ext[:, 2 - lag_tap : 2 - lag_tap + frame_count],
                grad_out,
                preferred_element_type=jnp.float32,
            )
            for lag_tap in range(3)
        ]
    )
    pixels = (
        clip_count
        * frame_count
        * row_count
        * col_count
        * lax.axis_size("dp")
        * lax.axis_size("tm")
        * lax.axis_size("height")
    )
    factor = 1.0 / math.sqrt(pixels)
    sigma = jax.nn.sigmoid(pre_act)
    grad_pre = (grad_hidden * sigma * (1.0 + pre_act * (1.0 - sigma))).astype(jnp.bfloat16)
    grad_rows = extended(grad_pre, (("height", 2),), 1)
    grad_stack = column_stack(grad_rows)
    grad_input = None
    for row_tap in range(3):
        back_matrix = jnp.concatenate(
            [w_spatial[row_tap, 2 - col_tap].T for col_tap in range(3)], axis=0
        )
        partial_value = jnp.einsum(
            "bfrwk,kd->bfrwd",
            grad_stack[:, :, 2 - row_tap : 2 - row_tap + row_count],
            back_matrix,
            preferred_element_type=jnp.float32,
        )
        grad_input = partial_value if grad_input is None else grad_input + partial_value
    grad_in = grad_input.astype(jnp.bfloat16)
    spatial_local = jnp.stack(
        [
            jnp.einsum(
                "bfrwk,bfrwd->kd",
                stacked[:, :, row_tap : row_tap + row_count],
                grad_pre,
                preferred_element_type=jnp.float32,
            ).reshape(3, channels, channels)
            for row_tap in range(3)
        ]
    )
    summed_spatial, summed_temporal = lax.psum(
        (spatial_local, temporal_local), ("dp", "tm", "height")
    )
    grad_spatial = summed_spatial * factor
    grad_temporal = summed_temporal * factor
    return (layer_out, grad_in, grad_spatial, grad_temporal)


def solution(mesh):
    in_specs = (P("dp", "tm", "height", None, None), P("dp", "tm", "height", None, None), P(), P())
    out_specs = (P("dp", "tm", "height", None, None), P("dp", "tm", "height", None, None), P(), P())
    return jax.shard_map(
        per_device, mesh=mesh, in_specs=in_specs, out_specs=out_specs, check_vma=False
    )
```

profile of v0, /device:TPU:1, one launch (start us, length us, event | category | flops | bytes accessed | tf_op | source)
XLA Modules:
  0.0 224.0 jit_solution(14255794308384720880)
XLA Ops:
  7.2 0.0 all-reduce.5.cloned.1.call-start
  7.2 2.0 fusion.69
  9.2 1.3 collective-permute-start.1
  10.5 5.4 %collective-permute-start = (bf16[1,3,1,320,128]{4,3,2,1,0:T(8,128)(2,1)}, bf16[1,3,1,320,128]{4,3,2,1,0:T(8,128)(2,1)}, u32[]{:S(2)}, u32[]{:S(2)}) collective-permute-start(bf16[1,3,1,320,128]{4,3,2,1,0:T(8,128)(2,1)} %get-tuple-element.16), channel_id=1, source_target_pairs={{0,1},{1,2},{2,3},{4,5},{5,6},{6,7},{8,9},{9,10},{10,11},{12,13},{... | collective-permute-start | bytes 737288 | tf_op jit(solution)/shard_map/ppermute | solution.py:16
  15.9 1.8 slice.131
  17.7 2.9 %collective-permute-start.3 = (bf16[1,2,3,320,128]{4,3,2,1,0:T(8,128)(2,1)}, bf16[1,2,3,320,128]{4,3,2,1,0:T(8,128)(2,1)}, u32[]{:S(2)}, u32[]{:S(2)}) collective-permute-start(bf16[1,2,3,320,128]{4,3,2,1,0:T(8,128)(2,1)} %slice.131), channel_id=1, source_target_pairs={{4,0},{8,4},{12,8},{5,1},{9,5},{13,9},{6,2},{10,6},{14,10},{7,3},{... | collective-permute-start | bytes 1474568 | tf_op jit(solution)/shard_map/ppermute | solution.py:25
  20.6 0.6 fusion.70
  21.2 1.5 fusion.30
  22.8 1.5 copy.60
  24.3 1.5 copy.61
  25.8 1.5 copy.59
  27.2 0.7 copy.58
  27.9 0.7 copy.57
  28.7 0.7 copy.56
  29.4 0.7 copy.55
  30.1 0.7 copy.54
  30.8 0.7 copy.62
  31.6 1.0 constant_dynamic-update-slice_fusion.2
  32.5 0.1 constant_dynamic-update-slice_fusion.1
  32.7 0.7 pad_slice_fusion.3
  33.4 0.6 pad_maximum_fusion
  34.0 0.7 fusion.6
  34.7 0.7 fusion.8
  35.5 0.4 copy-done.5
  35.8 0.8 copy-done.7
  36.7 2.0 multiply_convert_fusion.1
  38.7 3.1 %slice_bitcast_fusion.8 = (bf16[384,3,3,320]{0,3,2,1:T(8,128)(2,1)}, bf16[384,3,3,320]{0,3,2,1:T(8,128)(2,1)}, bf16[384,3,3,320]{0,3,2,1:T(8,128)(2,1)}) fusion(bf16[1,3,5,320,384]{4,3,2,1,0:T(8,128)(2,1)S(1)} %pad_maximum_fusion), kind=kLoop, calls=%fused_computation.21 | loop fusion | bytes 13271040 | tf_op jit(solution)/shard_map/bfrwk,bfrwd->kd/dot_general | solution.py:120
  41.8 0.8 slice.153
  42.6 3.5 %collective-permute-start.2 = (bf16[1,2,3,320,128]{4,3,2,1,0:T(8,128)(2,1)}, bf16[1,2,3,320,128]{4,3,2,1,0:T(8,128)(2,1)}, u32[]{:S(2)}, u32[]{:S(2)}) collective-permute-start(bf16[1,2,3,320,128]{4,3,2,1,0:T(8,128)(2,1)} %slice.153), channel_id=1, source_target_pairs={{0,4},{4,8},{8,12},{1,5},{5,9},{9,13},{2,6},{6,10},{10,14},{3,7},{... | collective-permute-start | bytes 1474568 | tf_op jit(solution)/shard_map/ppermute | solution.py:25
  46.1 5.6 %copy.29 = bf16[384,3,3,320]{3,0,2,1:T(8,128)(2,1)} copy(bf16[384,3,3,320]{0,3,2,1:T(8,128)(2,1)} %get-tuple-element.6) | data formatting | bytes 4423680 | tf_op jit(solution)/shard_map/bfrwk,bfrwd->kd/dot_general | solution.py:120
  51.7 5.7 %copy.31 = bf16[384,3,3,320]{3,0,2,1:T(8,128)(2,1)} copy(bf16[384,3,3,320]{0,3,2,1:T(8,128)(2,1)} %get-tuple-element.7) | data formatting | bytes 4423680 | tf_op jit(solution)/shard_map/bfrwk,bfrwd->kd/dot_general | solution.py:120
  57.4 5.6 %copy.33 = bf16[384,3,3,320]{3,0,2,1:T(8,128)(2,1)} copy(bf16[384,3,3,320]{0,3,2,1:T(8,128)(2,1)} %get-tuple-element.8) | data formatting | bytes 4423680 | tf_op jit(solution)/shard_map/bfrwk,bfrwd->kd/dot_general | solution.py:120
  63.0 0.4 convolution_bitcast_fusion.5
  63.5 1.5 fusion.52
  65.0 1.2 constant_dynamic-update-slice_fusion.3
  66.2 0.3 fusion.22
  66.6 0.4 copy-done.8
  67.0 0.8 multiply_convert_fusion
  67.9 2.5 %collective-permute-start.4 = (bf16[1,3,1,320,128]{4,3,2,1,0:T(8,128)(2,1)S(1)}, bf16[1,3,1,320,128]{4,3,2,1,0:T(8,128)(2,1)S(1)}, u32[]{:S(2)}, u32[]{:S(2)}) collective-permute-start(bf16[1,3,1,320,128]{4,3,2,1,0:T(8,128)(2,1)S(1)} %get-tuple-element.13), channel_id=1, source_target_pairs={{0,1},{1,2},{2,3},{4,5},{5,6},{6,7},{8,9},{9,10},{10,11},{12,13},{... | collective-permute-start | bytes 737288 | tf_op jit(solution)/shard_map/ppermute | solution.py:16
  70.4 1.5 collective-permute-start.5
  71.9 0.8 convolution_bitcast_fusion.2
  72.7 0.9 copy-done.2
  73.6 0.8 convolution_bitcast_fusion.1
  74.4 1.0 copy-done.3
  75.4 0.8 convolution_bitcast_fusion
  76.2 0.9 pad_maximum_fusion.3
  77.0 2.4 %collective-permute-done.5 = bf16[1,3,1,320,128]{4,3,2,1,0:T(8,128)(2,1)S(1)} collective-permute-done((bf16[1,3,1,320,128]{4,3,2,1,0:T(8,128)(2,1)S(1)}, bf16[1,3,1,320,128]{4,3,2,1,0:T(8,128)(2,1)S(1)}, u32[]{:S(2)}, u32[]{:S(2)}) %collective-permute-start.5) | collective-permute-done | bytes 245792 | tf_op jit(solution)/shard_map/ppermute | solution.py:17
  79.4 0.7 copy-done.13
  80.1 0.3 fusion.18
  80.4 1.8 fusion.67
  82.2 1.3 convolution_bitcast_fusion.4
  83.5 1.4 convolution_bitcast_fusion.3
  85.0 0.7 pad_maximum_fusion.4
  85.7 0.0 all-reduce.5.cloned.1.call-update
  85.7 1.8 pad_maximum_fusion.1
  87.6 0.7 fusion.2
  88.3 0.7 fusion.3
  89.1 1.4 fusion.49
  90.5 0.1 copy-done.4
  90.6 2.3 %fusion.16 = bf16[1,3,3,320,128]{4,3,2,1,0:T(8,128)(2,1)} fusion(f32[3,3,320,128]{3,2,1,0:T(8,128)S(1)} %copy-done.4, f32[3,3,320,128]{3,2,1,0:T(8,128)S(1)} %fusion.49, bf16[1,3,3,320,128]{4,3,2,1,0:T(8,128)(2,1)S(1)} %bitcast.209, bf16[1,2,3,320,128]{4,3,2,1,0:T(8,128)(2,1)} %collective-permute-done.2, bf16[3,128,128]{2,1,0:T(8,128)(2,1)S(1)} %copy-done.14), kind=kOutput, calls=%fused_computation.32 | convolution fusion | flops 95846400 | bytes 4947968 | tf_op jit(solution)/shard_map/bfrwc,cd->bfrwd/dot_general | solution.py:61
  92.8 1.6 fusion.21
  94.5 119.2 %all-reduce.5.cloned.1.call-done = (f32[3,3,128,128]{3,2,1,0:T(8,128)}, f32[3,128,128]{2,1,0:T(8,128)}) async-done(((f32[3,3,128,128]{3,2,1,0:T(8,128)}, f32[3,128,128]{2,1,0:T(8,128)}), (f32[3,3,128,128]{3,2,1,0:T(8,128)}, f32[3,128,128]{2,1,0:T(8,128)})) %all-reduce.5.cloned.1.call-update) | async-done | bytes 786448 | tf_op jit(solution)/shard_map/psum | solution.py:129
  213.6 1.9 broadcast_multiply_fusion
  215.6 1.6 broadcast_multiply_fusion.1
  (52 shorter events, 0.2 us)
Async XLA Ops:
  7.2 14.1 %copy-start = (bf16[1,3,3,320,128]{4,3,2,1,0:T(8,128)(2,1)S(1)}, bf16[1,3,3,320,128]{4,3,2,1,0:T(8,128)(2,1)}, u32[]{:S(2)}) copy-start(bf16[1,3,3,320,128]{4,3,2,1,0:T(8,128)(2,1)} %param.5) | copy-start | bytes 2211844
  7.2 13.4 %copy-start.11 = (bf16[3,3,128,128]{3,2,1,0:T(8,128)(2,1)S(1)}, bf16[3,3,128,128]{3,2,1,0:T(8,128)(2,1)}, u32[]{:S(2)}) copy-start(bf16[3,3,128,128]{3,2,1,0:T(8,128)(2,1)} %param.6) | copy-start | bytes 884740
  7.2 14.0 %copy-start.14 = (bf16[3,128,128]{2,1,0:T(8,128)(2,1)S(1)}, bf16[3,128,128]{2,1,0:T(8,128)(2,1)}, u32[]{:S(2)}) copy-start(bf16[3,128,128]{2,1,0:T(8,128)(2,1)} %param.7) | copy-start | bytes 294916
  7.2 206.4 %all-reduce.5.cloned.1.call-start = ((), (), s32[]{:S(2)}) async-start(), calls=%async_computation | async-start | bytes 1572864 | tf_op jit(solution)/shard_map/psum | solution.py:129
  9.2 23.5 %collective-permute-start.1 = (bf16[1,3,1,320,128]{4,3,2,1,0:T(8,128)(2,1)}, bf16[1,3,1,320,128]{4,3,2,1,0:T(8,128)(2,1)S(1)}, u32[]{:S(2)}, u32[]{:S(2)}) collective-permute-start(bf16[1,3,1,320,128]{4,3,2,1,0:T(8,128)(2,1)} %get-tuple-element.15), channel_id=1, source_target_pairs={{1,0},{2,1},{3,2},{5,4},{6,5},{7,6},{9,8},{10,9},{11,10},{13,12},{... | collective-permute-start | bytes 737288 | tf_op jit(solution)/shard_map/ppermute | solution.py:17
  10.5 21.1 %collective-permute-start = (bf16[1,3,1,320,128]{4,3,2,1,0:T(8,128)(2,1)}, bf16[1,3,1,320,128]{4,3,2,1,0:T(8,128)(2,1)}, u32[]{:S(2)}, u32[]{:S(2)}) collective-permute-start(bf16[1,3,1,320,128]{4,3,2,1,0:T(8,128)(2,1)} %get-tuple-element.16), channel_id=1, source_target_pairs={{0,1},{1,2},{2,3},{4,5},{5,6},{6,7},{8,9},{9,10},{10,11},{12,13},{... | collective-permute-start | bytes 737288 | tf_op jit(solution)/shard_map/ppermute | solution.py:16
  17.7 47.3 %collective-permute-start.3 = (bf16[1,2,3,320,128]{4,3,2,1,0:T(8,128)(2,1)}, bf16[1,2,3,320,128]{4,3,2,1,0:T(8,128)(2,1)}, u32[]{:S(2)}, u32[]{:S(2)}) collective-permute-start(bf16[1,2,3,320,128]{4,3,2,1,0:T(8,128)(2,1)} %slice.131), channel_id=1, source_target_pairs={{4,0},{8,4},{12,8},{5,1},{9,5},{13,9},{6,2},{10,6},{14,10},{7,3},{... | collective-permute-start | bytes 1474568 | tf_op jit(solution)/shard_map/ppermute | solution.py:25
  22.7 9.8 %copy-start.9 = (bf16[1,3,3,320,128]{4,3,2,1,0:T(8,128)(2,1)S(1)}, bf16[1,3,3,320,128]{4,3,2,1,0:T(8,128)(2,1)}, u32[]{:S(2)}) copy-start(bf16[1,3,3,320,128]{4,3,2,1,0:T(8,128)(2,1)} %param.4) | copy-start | bytes 2211844
  34.7 1.1 copy-start.5
  35.5 1.2 copy-start.7
  42.6 39.6 %collective-permute-start.2 = (bf16[1,2,3,320,128]{4,3,2,1,0:T(8,128)(2,1)}, bf16[1,2,3,320,128]{4,3,2,1,0:T(8,128)(2,1)}, u32[]{:S(2)}, u32[]{:S(2)}) collective-permute-start(bf16[1,2,3,320,128]{4,3,2,1,0:T(8,128)(2,1)} %slice.153), channel_id=1, source_target_pairs={{0,4},{4,8},{8,12},{1,5},{5,9},{9,13},{2,6},{6,10},{10,14},{3,7},{... | collective-permute-start | bytes 1474568 | tf_op jit(solution)/shard_map/ppermute | solution.py:25
  63.0 3.5 %copy-start.24 = (f32[3,3,320,128]{3,2,1,0:T(8,128)S(1)}, f32[3,3,320,128]{3,2,1,0:T(8,128)}, u32[]{:S(2)}) copy-start(f32[3,3,320,128]{3,2,1,0:T(8,128)} %get-tuple-element.30) | copy-start | bytes 4423684
  63.4 3.1 %copy-start.10 = (f32[3,3,320,128]{3,2,1,0:T(8,128)S(1)}, f32[3,3,320,128]{3,2,1,0:T(8,128)}, u32[]{:S(2)}) copy-start(f32[3,3,320,128]{3,2,1,0:T(8,128)} %fusion.30) | copy-start | bytes 4423684
  65.0 1.6 copy-start.6
  65.0 2.0 copy-start.8
  67.0 4.9 %copy-start.1 = (bf16[384,3,3,320]{3,0,2,1:T(8,128)(2,1)S(1)}, bf16[384,3,3,320]{3,0,2,1:T(8,128)(2,1)}, u32[]{:S(2)}) copy-start(bf16[384,3,3,320]{3,0,2,1:T(8,128)(2,1)} %copy.29) | copy-start | bytes 6635524
  67.9 9.2 %collective-permute-start.4 = (bf16[1,3,1,320,128]{4,3,2,1,0:T(8,128)(2,1)S(1)}, bf16[1,3,1,320,128]{4,3,2,1,0:T(8,128)(2,1)S(1)}, u32[]{:S(2)}, u32[]{:S(2)}) collective-permute-start(bf16[1,3,1,320,128]{4,3,2,1,0:T(8,128)(2,1)S(1)} %get-tuple-element.13), channel_id=1, source_target_pairs={{0,1},{1,2},{2,3},{4,5},{5,6},{6,7},{8,9},{9,10},{10,11},{12,13},{... | collective-permute-start | bytes 737288 | tf_op jit(solution)/shard_map/ppermute | solution.py:16
  70.4 9.0 %collective-permute-start.5 = (bf16[1,3,1,320,128]{4,3,2,1,0:T(8,128)(2,1)S(1)}, bf16[1,3,1,320,128]{4,3,2,1,0:T(8,128)(2,1)S(1)}, u32[]{:S(2)}, u32[]{:S(2)}) collective-permute-start(bf16[1,3,1,320,128]{4,3,2,1,0:T(8,128)(2,1)S(1)} %get-tuple-element.14), channel_id=1, source_target_pairs={{1,0},{2,1},{3,2},{5,4},{6,5},{7,6},{9,8},{10,9},{11,10},{13,12},{... | collective-permute-start | bytes 737288 | tf_op jit(solution)/shard_map/ppermute | solution.py:17
  71.9 1.8 copy-start.2
  73.6 1.7 copy-start.3
  77.0 2.4 %copy-start.12 = (bf16[1,3,1,320,128]{4,3,2,1,0:T(8,128)(2,1)}, bf16[1,3,1,320,128]{4,3,2,1,0:T(8,128)(2,1)S(1)}, u32[]{:S(2)}) copy-start(bf16[1,3,1,320,128]{4,3,2,1,0:T(8,128)(2,1)S(1)} %collective-permute-done.4) | copy-start | bytes 737284
  79.4 0.7 copy-start.13
  85.7 1.8 copy-start.18
  85.7 1.8 copy-start.19
  85.7 1.8 copy-start.20
  87.5 0.8 copy-start.21
  87.5 0.8 copy-start.22
  87.6 0.8 copy-start.23
  89.1 1.5 copy-start.4
  90.6 2.3 %copy-start.15 = (bf16[1,1,128,128]{2,3,1,0:T(8,128)(2,1)S(1)}, bf16[1,1,128,128]{2,3,1,0:T(8,128)(2,1)}, u32[]{:S(2)}) copy-start(bf16[1,1,128,128]{2,3,1,0:T(8,128)(2,1)} %copy.60) | copy-start | bytes 98308
  90.6 2.3 %copy-start.16 = (bf16[1,1,128,128]{2,3,1,0:T(8,128)(2,1)S(1)}, bf16[1,1,128,128]{2,3,1,0:T(8,128)(2,1)}, u32[]{:S(2)}) copy-start(bf16[1,1,128,128]{2,3,1,0:T(8,128)(2,1)} %copy.61) | copy-start | bytes 98308
  90.6 2.3 %copy-start.17 = (bf16[1,1,128,128]{2,3,1,0:T(8,128)(2,1)S(1)}, bf16[1,1,128,128]{2,3,1,0:T(8,128)(2,1)}, u32[]{:S(2)}) copy-start(bf16[1,1,128,128]{2,3,1,0:T(8,128)(2,1)} %copy.62) | copy-start | bytes 98308
Sparse Core Ops, SparseCore 0:
  85.8 127.7 all-reduce.4
where the time goes:
time: 227 us; the launch traced here: 224 us
  waiting for transfers between devices  122 us (54%)
  local copies, waits for them, and re-layouts  43.3 us (19%)
  matrix products  19.9 us (9%)
  starting transfers between devices  17 us (7%)
  between operations  14.5 us (6%)
  other arithmetic  7.8 us (3%)
    psum x1, waiting for transfers between devices, per_device(): lax.psum((spatial_local, temporal_local), ('dp', 'tm', 'height'))  119 us
    dot_general x4, local copies, waits for them, and re-layouts, per_device(): jnp.einsum('bfrwk,bfrwd->kd', stacked[:, :, row_tap:row_tap + row_count],...  20.1 us
    unnamed x62, local copies, waits for them, and re-layouts  14.3 us
    ppermute x2, starting transfers between devices, extended(): before = lax.ppermute(last, axis, up)  7.9 us
    ppermute x2, starting transfers between devices, shifted(): return lax.ppermute(value, axis, pairs)  6.31 us
    dot_general x3, matrix products, per_device(): jnp.einsum('bfrwc,cd->bfrwd', hidden_ext[:, 2 - lag_tap:2 - lag_tap + fra...  5.14 us
  transfers between devices with their start and end apart: 7, of which 2 were waited for; matrix products, arithmetic and copies ran while one was open for 26% of the time, Pallas kernels for 0%

commit v1 on v0

v1 whole, which is shorter than its diff:
```python
import functools
import math

import jax
import jax.numpy as jnp
from jax import lax
from jax.experimental import pallas as pl
from jax.experimental.pallas import tpu as pltpu
from jax.sharding import PartitionSpec as P

F32, BF16 = jnp.float32, jnp.bfloat16


def tdot(lhs, rhs):
    return lax.dot_general(lhs, rhs, (((0,), (0,)), ((), ())), preferred_element_type=F32)


def dot(lhs, rhs):
    return jnp.dot(lhs, rhs, preferred_element_type=F32)


def kernel(
    sizes, dims, factor,
    x_hbm, g_hbm, ws_ref, wt_ref,
    lo_hbm, gi_hbm, res_hbm,
    x_ext, xs, g_ext, hid, gp, gps, wb, wtb, acc, part, rs1, s1, rs2, dps, res, lo, gi,
    loc, xh_s, xh_r, gh_s, gh_r, hd_s, hd_r, gp_s, gp_r,
    rs1_s, rs1_r, rs2_s, rs2_r, dp_s, dp_r, ag1_s, ag1_r, ag2_s, ag2_r,
):
    n_dp, n_tm, n_h = sizes
    frames, rows, cols, ch = dims
    pix = rows * cols
    total = 12 * ch
    chunk = total // n_tm
    piece = chunk // n_h
    spatial_chunks = (9 * ch) // chunk
    me_dp, me_tm, me_h = lax.axis_index("dp"), lax.axis_index("tm"), lax.axis_index("height")

    def remote(src, dst, send, recv, axis, peer):
        return pltpu.make_async_remote_copy(
            src_ref=src, dst_ref=dst, send_sem=send, recv_sem=recv,
            device_id={axis: peer}, device_id_type=pl.DeviceIdType.MESH,
        )

    x_in = pltpu.make_async_copy(x_hbm.at[0], x_ext.at[:, pl.ds(1, rows)], loc.at[0])
    g_in = pltpu.make_async_copy(g_hbm.at[0], g_ext.at[pl.ds(0, frames)], loc.at[1])
    x_in.start()
    g_in.start()

    barrier = pltpu.get_barrier_semaphore()
    axes = (("dp", n_dp, me_dp), ("tm", n_tm, me_tm), ("height", n_h, me_h))
    for axis, count, me in axes:
        for step in range(1, count):
            pl.semaphore_signal(
                barrier, inc=1, device_id={axis: lax.rem(me + step, count)},
                device_id_type=pl.DeviceIdType.MESH,
            )
    pl.semaphore_wait(barrier, n_dp + n_tm + n_h - 3)

    has_up, has_down = me_h > 0, me_h < n_h - 1
    has_prev, has_next = me_tm > 0, me_tm < n_tm - 1
    up, down = lax.rem(me_h + n_h - 1, n_h), lax.rem(me_h + 1, n_h)
    prev, nxt = lax.rem(me_tm + n_tm - 1, n_tm), lax.rem(me_tm + 1, n_tm)

    x_down = remote(x_hbm.at[0, :, rows - 1], x_ext.at[:, 0], xh_s.at[0], xh_r.at[0], "height", down)
    x_up = remote(x_hbm.at[0, :, 0], x_ext.at[:, rows + 1], xh_s.at[1], xh_r.at[1], "height", up)
    g_prev = remote(
        g_hbm.at[0, pl.ds(0, 2)], g_ext.at[pl.ds(frames, 2)], gh_s.at[0], gh_r.at[0], "tm", prev
    )
    pl.when(has_down)(x_down.start)
    pl.when(has_up)(x_up.start)
    pl.when(has_prev)(g_prev.start)

    @pl.when(me_h == 0)
    def _():
        x_ext[:, 0] = jnp.zeros((frames, cols, ch), BF16)
        gp[:, 0] = jnp.zeros((frames, cols, ch), BF16)

    @pl.when(me_h == n_h - 1)
    def _():
        x_ext[:, rows + 1] = jnp.zeros((frames, cols, ch), BF16)
        gp[:, rows + 1] = jnp.zeros((frames, cols, ch), BF16)

    @pl.when(me_tm == 0)
    def _():
        hid[pl.ds(0, 2)] = jnp.zeros((2, rows, cols, ch), BF16)

    @pl.when(me_tm == n_tm - 1)
    def _():
        g_ext[pl.ds(frames, 2)] = jnp.zeros((2, rows, cols, ch), BF16)

    for i in range(3):
        for j in range(3):
            wb[i, pl.ds((2 - j) * ch, ch)] = ws_ref[i, j].T
        wtb[pl.ds(i * ch, ch)] = wt_ref[i].T

    place = lax.broadcasted_iota(jnp.int32, (cols, ch), 0)

    def stack(source, target, f, r):
        value = source[f, r]
        wide = value.astype(F32)
        left = jnp.where(place == 0, 0.0, pltpu.roll(wide, 1, 0))
        right = jnp.where(place == cols - 1, 0.0, pltpu.roll(wide, cols - 1, 0))
        target[f, r, :, pl.ds(0, ch)] = left.astype(BF16)
        target[f, r, :, pl.ds(ch, ch)] = value
        target[f, r, :, pl.ds(2 * ch, ch)] = right.astype(BF16)

    x_in.wait()

    @pl.loop(0, frames)
    def _(f):
        for r in range(1, rows + 1):
            stack(x_ext, xs, f, r)

    g_in.wait()
    pl.when(has_up)(x_down.wait_recv)
    pl.when(has_down)(x_up.wait_recv)

    @pl.loop(0, frames)
    def _(f):
        for r in (0, rows + 1):
            stack(x_ext, xs, f, r)

    pl.when(has_next)(g_prev.wait_recv)

    def h_copy(f):
        return remote(
            hid.at[f + 2], hid.at[f + 2 - frames],
            hd_s.at[f], hd_r.at[f], "tm", nxt,
        )

    def p_copy(f, side):
        if side == 0:
            return remote(gp.at[f, rows], gp.at[f, 0], gp_s.at[f, 0], gp_r.at[f, 0], "height", down)
        return remote(gp.at[f, 1], gp.at[f, rows + 1], gp_s.at[f, 1], gp_r.at[f, 1], "height", up)

    def three(source, f0, f1, f2):
        return jnp.concatenate(
            [source[f].reshape(pix, ch) for f in (f0, f1, f2)], axis=1
        )

    @pl.loop(0, frames)
    def _(step):
        f = frames - 1 - step
        pre = None
        for i in range(3):
            term = dot(
                xs[f, pl.ds(i, rows)].reshape(pix, 3 * ch), ws_ref[i].reshape(3 * ch, ch)
            )
            pre = term if pre is None else pre + term
        sigma = jax.nn.sigmoid(pre)
        hid[f + 2] = (pre * sigma).astype(BF16).reshape(rows, cols, ch)

        @pl.when(jnp.logical_and(f >= frames - 2, has_next))
        def _():
            h_copy(f).start()

        grad_hidden = dot(three(g_ext, f, f + 1, f + 2), wtb[...])
        grad_pre = grad_hidden * sigma * (1.0 + pre * (1.0 - sigma))
        gp[f, pl.ds(1, rows)] = grad_pre.astype(BF16).reshape(rows, cols, ch)
        pl.when(has_down)(p_copy(f, 0).start)
        pl.when(has_up)(p_copy(f, 1).start)
        for r in range(1, rows + 1):
            stack(gp, gps, f, r)

    acc[...] = jnp.zeros((total, ch), F32)

    @pl.loop(0, frames)
    def _(f):
        right = gps[f, pl.ds(1, rows)].reshape(pix, 3 * ch)
        for i in range(3):
            term = tdot(x_ext[f, pl.ds(i, rows)].reshape(pix, ch), right)
            for j in range(3):
                acc[pl.ds((3 * i + j) * ch, ch)] += term[:, (2 - j) * ch : (3 - j) * ch]

    part[pl.ds(0, 9 * ch)] = acc[pl.ds(0, 9 * ch)].astype(BF16)

    def rs1_copy(step):
        peer = lax.rem(me_tm + step, n_tm)
        return peer, remote(
            part.at[pl.ds(pl.multiple_of(peer * chunk, chunk), chunk)], rs1.at[step - 1],
            rs1_s.at[step - 1], rs1_r.at[step - 1], "tm", peer,
        )

    for step in range(1, n_tm):
        peer, copy = rs1_copy(step)
        pl.when(peer < spatial_chunks)(copy.start)

    @pl.when(has_prev)
    def _():
        for f in (frames - 1, frames - 2):
            h_copy(f).wait_recv()

    @pl.loop(0, frames)
    def _(f):
        back = three(hid, f + 2, f + 1, f)
        acc[pl.ds(9 * ch, 3 * ch)] += tdot(back, g_ext[f].reshape(pix, ch))

    part[pl.ds(9 * ch, 3 * ch)] = acc[pl.ds(9 * ch, 3 * ch)].astype(BF16)
    for step in range(1, n_tm):
        peer, copy = rs1_copy(step)
        pl.when(peer >= spatial_chunks)(copy.start)

    @pl.loop(0, frames)
    def _(f):
        mixed = dot(three(hid, f + 2, f + 1, f), wt_ref[...].reshape(3 * ch, ch))
        lo[f] = mixed.astype(BF16).reshape(rows, cols, ch)

    lo_out = pltpu.make_async_copy(lo, lo_hbm.at[0], loc.at[2])
    lo_out.start()

    summed = acc[pl.ds(pl.multiple_of(me_tm * chunk, chunk), chunk)]
    for step in range(1, n_tm):
        rs1_copy(step)[1].wait_recv()
        summed = summed + rs1[step - 1].astype(F32)
    acc[pl.ds(0, chunk)] = summed
    s1[...] = summed.astype(BF16)

    def rs2_copy(step):
        peer = lax.rem(me_h + step, n_h)
        return remote(
            s1.at[pl.ds(pl.multiple_of(peer * piece, piece), piece)], rs2.at[step - 1],
            rs2_s.at[step - 1], rs2_r.at[step - 1], "height", peer,
        )

    for step in range(1, n_h):
        rs2_copy(step).start()

    def gi_copy(f):
        return pltpu.make_async_copy(gi.at[f], gi_hbm.at[0, f], loc.at[3 + f])

    def grad_in(f):
        @pl.when(has_up)
        def _():
            p_copy(f, 0).wait_recv()

        @pl.when(has_down)
        def _():
            p_copy(f, 1).wait_recv()

        for r in (0, rows + 1):
            stack(gp, gps, f, r)
        value = None
        for i in range(3):
            term = dot(gps[f, pl.ds(2 - i, rows)].reshape(pix, 3 * ch), wb[i])
            value = term if value is None else value + term
        gi[f] = value.astype(BF16).reshape(rows, cols, ch)
        gi_copy(f).start()

    pl.loop(frames - 2, frames)(grad_in)

    own = acc[pl.ds(pl.multiple_of(me_h * piece, piece), piece)]
    for step in range(1, n_h):
        rs2_copy(step).wait_recv()
        own = own + rs2[step - 1].astype(F32)
    dps[me_dp] = own

    def dp_copy(step):
        peer = lax.rem(me_dp + step, n_dp)
        return remote(
            dps.at[me_dp], dps.at[me_dp], dp_s.at[step - 1], dp_r.at[me_dp], "dp", peer
        )

    def dp_from(step):
        src = lax.rem(me_dp + n_dp - step, n_dp)
        return remote(dps.at[src], dps.at[src], dp_s.at[step - 1], dp_r.at[src], "dp", src)

    for step in range(1, n_dp):
        dp_copy(step).start()

    pl.loop(0, frames - 2)(grad_in)

    for step in range(1, n_dp):
        dp_from(step).wait_recv()
    whole = dps[0]
    for d in range(1, n_dp):
        whole = whole + dps[d]
    base = pl.multiple_of(me_tm * chunk + me_h * piece, piece)
    res[pl.ds(base, piece)] = (whole * factor).astype(BF16)

    def ag1_copy(step):
        peer = lax.rem(me_h + step, n_h)
        at = res.at[pl.ds(base, piece)]
        return remote(at, at, ag1_s.at[step - 1], ag1_r.at[step - 1], "height", peer)

    def ag1_from(step):
        src = lax.rem(me_h + n_h - step, n_h)
        at = res.at[pl.ds(pl.multiple_of(me_tm * chunk + src * piece, piece), piece)]
        return remote(at, at, ag1_s.at[step - 1], ag1_r.at[step - 1], "height", src)

    for step in range(1, n_h):
        ag1_copy(step).start()
    for step in range(1, n_h):
        ag1_from(step).wait_recv()

    def ag2_copy(step):
        peer = lax.rem(me_tm + step, n_tm)
        at = res.at[pl.ds(pl.multiple_of(me_tm * chunk, chunk), chunk)]
        return remote(at, at, ag2_s.at[step - 1], ag2_r.at[step - 1], "tm", peer)

    def ag2_from(step):
        src = lax.rem(me_tm + n_tm - step, n_tm)
        at = res.at[pl.ds(pl.multiple_of(src * chunk, chunk), chunk)]
        return remote(at, at, ag2_s.at[step - 1], ag2_r.at[step - 1], "tm", src)

    for step in range(1, n_tm):
        ag2_copy(step).start()
    for step in range(1, n_tm):
        ag2_from(step).wait_recv()
    res_out = pltpu.make_async_copy(res, res_hbm, loc.at[3 + frames])
    res_out.start()

    pl.when(has_down)(x_down.wait_send)
    pl.when(has_up)(x_up.wait_send)
    pl.when(has_prev)(g_prev.wait_send)

    @pl.when(has_next)
    def _():
        for f in (frames - 1, frames - 2):
            h_copy(f).wait_send()

    for f in range(frames):
        pl.when(has_down)(p_copy(f, 0).wait_send)
        pl.when(has_up)(p_copy(f, 1).wait_send)
    for step in range(1, n_tm):
        rs1_copy(step)[1].wait_send()
        ag2_copy(step).wait_send()
    for step in range(1, n_h):
        rs2_copy(step).wait_send()
        ag1_copy(step).wait_send()
    for step in range(1, n_dp):
        dp_copy(step).wait_send()
    lo_out.wait()
    for f in range(frames):
        gi_copy(f).wait()
    res_out.wait()


def per_device(sizes, frames_in, grad_out, w_spatial, w_temporal):
    clips, frames, rows, cols, ch = frames_in.shape
    n_dp, n_tm, n_h = sizes
    assert clips == 1 and (12 * ch) % (n_tm * n_h) == 0
    chunk = 12 * ch // n_tm
    piece = chunk // n_h
    factor = 1.0 / math.sqrt(clips * frames * rows * cols * n_dp * n_tm * n_h)
    any_spec = pl.BlockSpec(memory_space=pl.ANY)
    vmem_spec = pl.BlockSpec(memory_space=pltpu.VMEM)
    dma = pltpu.SemaphoreType.DMA
    layer_out, grad_in, sums = pl.pallas_call(
        functools.partial(kernel, sizes, (frames, rows, cols, ch), factor),
        out_shape=(
            jax.ShapeDtypeStruct(frames_in.shape, BF16),
            jax.ShapeDtypeStruct(frames_in.shape, BF16),
            jax.ShapeDtypeStruct((12 * ch, ch), BF16),
        ),
        in_specs=[any_spec, any_spec, vmem_spec, vmem_spec],
        out_specs=(any_spec, any_spec, any_spec),
        scratch_shapes=[
            pltpu.VMEM((frames, rows + 2, cols, ch), BF16),
            pltpu.VMEM((frames, rows + 2, cols, 3 * ch), BF16),
            pltpu.VMEM((frames + 2, rows, cols, ch), BF16),
            pltpu.VMEM((frames + 2, rows, cols, ch), BF16),
            pltpu.VMEM((frames, rows + 2, cols, ch), BF16),
            pltpu.VMEM((frames, rows + 2, cols, 3 * ch), BF16),
            pltpu.VMEM((3, 3 * ch, ch), BF16),
            pltpu.VMEM((3 * ch, ch), BF16),
            pltpu.VMEM((12 * ch, ch), F32),
            pltpu.VMEM((12 * ch, ch), BF16),
            pltpu.VMEM((n_tm - 1, chunk, ch), BF16),
            pltpu.VMEM((chunk, ch), BF16),
            pltpu.VMEM((n_h - 1, piece, ch), BF16),
            pltpu.VMEM((n_dp, piece, ch), F32),
            pltpu.VMEM((12 * ch, ch), BF16),
            pltpu.VMEM((frames, rows, cols, ch), BF16),
            pltpu.VMEM((frames, rows, cols, ch), BF16),
            dma((4 + frames,)),
            dma((2,)), dma((2,)), dma((1,)), dma((1,)),
            dma((frames,)), dma((frames,)), dma((frames, 2)), dma((frames, 2)),
            dma((n_tm - 1,)), dma((n_tm - 1,)), dma((n_h - 1,)), dma((n_h - 1,)),
            dma((n_dp,)), dma((n_dp,)),
            dma((n_h - 1,)), dma((n_h - 1,)), dma((n_tm - 1,)), dma((n_tm - 1,)),
        ],
        compiler_params=pltpu.CompilerParams(
            collective_id=0, has_side_effects=True, vmem_limit_bytes=48 << 20
        ),
    )(frames_in, grad_out, w_spatial, w_temporal)
    sums = sums.astype(F32)
    return (
        layer_out,
        grad_in,
        sums[: 9 * ch].reshape(3, 3, ch, ch),
        sums[9 * ch :].reshape(3, ch, ch),
    )


def solution(mesh):
    sizes = (mesh.shape["dp"], mesh.shape["tm"], mesh.shape["height"])
    spec = P("dp", "tm", "height", None, None)
    return jax.shard_map(
        functools.partial(per_device, sizes), mesh=mesh,
        in_specs=(spec, spec, P(), P()), out_specs=(spec, spec, P(), P()), check_vma=False,
    )
```

time: 227 us -> 50.4 us (0.22); the launches traced: 224 us -> 50.2 us
  waiting for transfers between devices: 122 us -> 0 us
  Pallas kernels: 0 us -> 42.2 us
  local copies, waits for them, and re-layouts: 43.3 us -> 7.35 us
  matrix products: 19.9 us -> 0 us
  starting transfers between devices: 17 us -> 0 us
  between operations: 14.5 us -> 0.65 us
  other arithmetic: 7.8 us -> 0 us
    psum x1 -> x0, waiting for transfers between devices: 119 us -> none  [per_device(): lax.psum((spatial_local, temporal_local), ('dp', 'tm', 'height'))]
    pallas_call x0 -> x1, Pallas kernels: none -> 42.2 us  [per_device(): pl.pallas_call(functools.partial(kernel, sizes, (frames, rows, cols, ch),...]
    dot_general x4 -> x0, local copies, waits for them, and re-layouts: 20.1 us -> none  [per_device(): jnp.einsum('bfrwk,bfrwd->kd', stacked[:, :, row_tap:row_tap + row_count],...]
    dot_general x18 -> x0, matrix products: 19.9 us -> none  [the longest x3 5.14 us: per_device(): jnp.einsum('bfrwc,cd->bfrwd', hidden_ext[:, 2 - lag_tap:2 - lag_tap + fra...]
    ppermute x6 -> x0, starting transfers between devices: 17 us -> none  [the longest x2 7.9 us: extended(): before = lax.ppermute(last, axis, up)]
    unnamed x62 -> x10, local copies, waits for them, and re-layouts: 14.3 us -> 5.8 us
    slice x8 -> x2, local copies, waits for them, and re-layouts: 7.73 us -> 1.55 us  [the longest x1 0.85 us: per_device(): sums[:9 * ch].reshape(3, 3, ch, ch)]
    mul x2 -> x0, other arithmetic: 3.55 us -> none  [the longest x1 1.93 us: per_device(): grad_spatial = summed_spatial * factor]
  transfers between devices with their start and end apart: 7 -> 0, of which waited for: 2 -> 0; matrix products, arithmetic and copies ran while one was open for 26% -> 0% of each run, Pallas kernels for 0% -> 0%
where the time goes in v1:
time: 50.4 us; the launch traced here: 50.2 us
  Pallas kernels  42.2 us (84%)
  local copies, waits for them, and re-layouts  7.35 us (15%)
  between operations  0.65 us (1%)
    pallas_call x1, Pallas kernels, per_device(): pl.pallas_call(functools.partial(kernel, sizes, (frames, rows, cols, ch),...  42.2 us
    unnamed x10, local copies, waits for them, and re-layouts  5.8 us

profile of v1, /device:TPU:1, one launch (start us, length us, event | category | flops | bytes accessed | tf_op | source)
XLA Modules:
  0.0 50.2 jit_solution(5088376851235517242)
XLA Ops:
  0.6 0.0 copy-start
  0.6 1.1 %copy-done = bf16[1,3,3,320,128]{4,3,2,1,0:T(8,128)(2,1)S(1)} copy-done((bf16[1,3,3,320,128]{4,3,2,1,0:T(8,128)(2,1)S(1)}, bf16[1,3,3,320,128]{4,3,2,1,0:T(8,128)(2,1)}, u32[]{:S(2)}) %copy-start) | copy-done | bytes 737304
  1.7 0.0 copy-start.1
  1.8 1.1 %copy-done.1 = bf16[1,3,3,320,128]{4,3,2,1,0:T(8,128)(2,1)S(1)} copy-done((bf16[1,3,3,320,128]{4,3,2,1,0:T(8,128)(2,1)S(1)}, bf16[1,3,3,320,128]{4,3,2,1,0:T(8,128)(2,1)}, u32[]{:S(2)}) %copy-start.1) | copy-done | bytes 737304
  2.9 0.0 copy-start.2
  2.9 1.0 %copy-done.2 = bf16[3,3,128,128]{3,2,1,0:T(8,128)(2,1)S(1)} copy-done((bf16[3,3,128,128]{3,2,1,0:T(8,128)(2,1)S(1)}, bf16[3,3,128,128]{3,2,1,0:T(8,128)(2,1)}, u32[]{:S(2)}) %copy-start.2) | copy-done | bytes 294936
  3.8 0.0 copy-start.3
  3.8 0.9 %copy-done.3 = bf16[3,128,128]{2,1,0:T(8,128)(2,1)S(1)} copy-done((bf16[3,128,128]{2,1,0:T(8,128)(2,1)S(1)}, bf16[3,128,128]{2,1,0:T(8,128)(2,1)}, u32[]{:S(2)}) %copy-start.3) | copy-done | bytes 98328
  4.7 42.2 %shard_map.75 = (bf16[1,3,3,320,128]{4,3,2,1,0:T(8,128)(2,1)S(1)}, bf16[1,3,3,320,128]{4,3,2,1,0:T(8,128)(2,1)S(1)}, bf16[1536,128]{1,0:T(8,128)(2,1)S(1)}) custom-call(bf16[1,3,3,320,128]{4,3,2,1,0:T(8,128)(2,1)S(1)} %copy-done, bf16[1,3,3,320,128]{4,3,2,1,0:T(8,128)(2,1)S(1)} %copy-done.1, bf16[3,3,128,128]{3,2,1,0:T(8,128)(2,1)S(1)} %copy-done.2, ...), custom_call_target="tpu_custom_call" | custom-call | tf_op jit(solution)/shard_map/pallas_call | solution.py:349
  46.9 0.9 %slice.8 = f32[1152,128]{1,0:T(8,128)} slice(bf16[1536,128]{1,0:T(8,128)(2,1)S(1)} %get-tuple-element.9), slice={[0:1152], [0:128]} | slice | bytes 1179648 | tf_op jit(solution)/shard_map/slice | solution.py:391
  47.7 0.7 %slice.9 = f32[384,128]{1,0:T(8,128)} slice(bf16[1536,128]{1,0:T(8,128)(2,1)S(1)} %get-tuple-element.9), slice={[1152:1536], [0:128]} | slice | bytes 393216 | tf_op jit(solution)/shard_map/slice | solution.py:392
  48.4 0.9 %copy.10 = bf16[1,3,3,320,128]{4,3,2,1,0:T(8,128)(2,1)} copy(bf16[1,3,3,320,128]{4,3,2,1,0:T(8,128)(2,1)S(1)} %get-tuple-element.14) | data formatting | bytes 1474560
  49.3 0.9 %copy.11 = bf16[1,3,3,320,128]{4,3,2,1,0:T(8,128)(2,1)} copy(bf16[1,3,3,320,128]{4,3,2,1,0:T(8,128)(2,1)S(1)} %get-tuple-element.15) | data formatting | bytes 1474560
Async XLA Ops:
  0.6 1.1 %copy-start = (bf16[1,3,3,320,128]{4,3,2,1,0:T(8,128)(2,1)S(1)}, bf16[1,3,3,320,128]{4,3,2,1,0:T(8,128)(2,1)}, u32[]{:S(2)}) copy-start(bf16[1,3,3,320,128]{4,3,2,1,0:T(8,128)(2,1)} %x_hbm.1) | copy-start | bytes 2211844
  1.7 1.1 %copy-start.1 = (bf16[1,3,3,320,128]{4,3,2,1,0:T(8,128)(2,1)S(1)}, bf16[1,3,3,320,128]{4,3,2,1,0:T(8,128)(2,1)}, u32[]{:S(2)}) copy-start(bf16[1,3,3,320,128]{4,3,2,1,0:T(8,128)(2,1)} %g_hbm.1) | copy-start | bytes 2211844
  2.9 1.0 %copy-start.2 = (bf16[3,3,128,128]{3,2,1,0:T(8,128)(2,1)S(1)}, bf16[3,3,128,128]{3,2,1,0:T(8,128)(2,1)}, u32[]{:S(2)}) copy-start(bf16[3,3,128,128]{3,2,1,0:T(8,128)(2,1)} %ws_ref.1) | copy-start | bytes 884740
  3.8 0.9 %copy-start.3 = (bf16[3,128,128]{2,1,0:T(8,128)(2,1)S(1)}, bf16[3,128,128]{2,1,0:T(8,128)(2,1)}, u32[]{:S(2)}) copy-start(bf16[3,128,128]{2,1,0:T(8,128)(2,1)} %wt_ref.1) | copy-start | bytes 294916

commit v2 on v1

--- a/solution.py
+++ b/solution.py
@@ -21,9 +21,9 @@
 
 def kernel(
     sizes, dims, factor,
-    x_hbm, g_hbm, ws_ref, wt_ref,
+    x_hbm, g_hbm, ws_hbm, wt_hbm,
     lo_hbm, gi_hbm, res_hbm,
-    x_ext, xs, g_ext, hid, gp, gps, wb, wtb, acc, part, rs1, s1, rs2, dps, res, lo, gi,
+    ws_ref, wt_ref, x_ext, xs, g_ext, hid, gp, gps, wb, wtb, acc, part, rs1, s1, rs2, dps, res, lo, gi,
     loc, xh_s, xh_r, gh_s, gh_r, hd_s, hd_r, gp_s, gp_r,
     rs1_s, rs1_r, rs2_s, rs2_r, dp_s, dp_r, ag1_s, ag1_r, ag2_s, ag2_r,
 ):
@@ -44,7 +44,11 @@
 
     x_in = pltpu.make_async_copy(x_hbm.at[0], x_ext.at[:, pl.ds(1, rows)], loc.at[0])
     g_in = pltpu.make_async_copy(g_hbm.at[0], g_ext.at[pl.ds(0, frames)], loc.at[1])
+    ws_in = pltpu.make_async_copy(ws_hbm, ws_ref, loc.at[4 + frames])
+    wt_in = pltpu.make_async_copy(wt_hbm, wt_ref, loc.at[5 + frames])
     x_in.start()
+    ws_in.start()
+    wt_in.start()
     g_in.start()
 
     barrier = pltpu.get_barrier_semaphore()
@@ -55,21 +59,25 @@
                 barrier, inc=1, device_id={axis: lax.rem(me + step, count)},
                 device_id_type=pl.DeviceIdType.MESH,
             )
-    pl.semaphore_wait(barrier, n_dp + n_tm + n_h - 3)
 
     has_up, has_down = me_h > 0, me_h < n_h - 1
     has_prev, has_next = me_tm > 0, me_tm < n_tm - 1
     up, down = lax.rem(me_h + n_h - 1, n_h), lax.rem(me_h + 1, n_h)
     prev, nxt = lax.rem(me_tm + n_tm - 1, n_tm), lax.rem(me_tm + 1, n_tm)
 
-    x_down = remote(x_hbm.at[0, :, rows - 1], x_ext.at[:, 0], xh_s.at[0], xh_r.at[0], "height", down)
-    x_up = remote(x_hbm.at[0, :, 0], x_ext.at[:, rows + 1], xh_s.at[1], xh_r.at[1], "height", up)
-    g_prev = remote(
-        g_hbm.at[0, pl.ds(0, 2)], g_ext.at[pl.ds(frames, 2)], gh_s.at[0], gh_r.at[0], "tm", prev
-    )
-    pl.when(has_down)(x_down.start)
-    pl.when(has_up)(x_up.start)
-    pl.when(has_prev)(g_prev.start)
+    def x_copy(f, side):
+        if side == 0:
+            return remote(
+                x_hbm.at[0, f, rows - 1], x_ext.at[f, 0],
+                xh_s.at[f, 0], xh_r.at[f, 0], "height", down,
+            )
+        return remote(
+            x_hbm.at[0, f, 0], x_ext.at[f, rows + 1],
+            xh_s.at[f, 1], xh_r.at[f, 1], "height", up,
+        )
+
+    def g_copy(f):
+        return remote(g_hbm.at[0, f], g_ext.at[frames + f], gh_s.at[f], gh_r.at[f], "tm", prev)
 
     @pl.when(me_h == 0)
     def _():
@@ -88,11 +96,6 @@
     @pl.when(me_tm == n_tm - 1)
     def _():
         g_ext[pl.ds(frames, 2)] = jnp.zeros((2, rows, cols, ch), BF16)
-
-    for i in range(3):
-        for j in range(3):
-            wb[i, pl.ds((2 - j) * ch, ch)] = ws_ref[i, j].T
-        wtb[pl.ds(i * ch, ch)] = wt_ref[i].T
 
     place = lax.broadcasted_iota(jnp.int32, (cols, ch), 0)
 
@@ -112,16 +115,20 @@
         for r in range(1, rows + 1):
             stack(x_ext, xs, f, r)
 
+    ws_in.wait()
+    wt_in.wait()
+    for i in range(3):
+        for j in range(3):
+            wb[i, pl.ds((2 - j) * ch, ch)] = ws_ref[i, j].T
+        wtb[pl.ds(i * ch, ch)] = wt_ref[i].T
     g_in.wait()
-    pl.when(has_up)(x_down.wait_recv)
-    pl.when(has_down)(x_up.wait_recv)
-
-    @pl.loop(0, frames)
-    def _(f):
-        for r in (0, rows + 1):
-            stack(x_ext, xs, f, r)
-
-    pl.when(has_next)(g_prev.wait_recv)
+
+    pl.semaphore_wait(barrier, n_dp + n_tm + n_h - 3)
+    for f in range(frames):
+        pl.when(has_down)(x_copy(f, 0).start)
+        pl.when(has_up)(x_copy(f, 1).start)
+    for f in range(2):
+        pl.when(has_prev)(g_copy(f).start)
 
     def h_copy(f):
         return remote(
@@ -140,8 +147,17 @@
         )
 
     @pl.loop(0, frames)
-    def _(step):
-        f = frames - 1 - step
+    def _(f):
+        @pl.when(has_up)
+        def _():
+            x_copy(f, 0).wait_recv()
+
+        @pl.when(has_down)
+        def _():
+            x_copy(f, 1).wait_recv()
+
+        for r in (0, rows + 1):
+            stack(x_ext, xs, f, r)
         pre = None
         for i in range(3):
             term = dot(
@@ -155,6 +171,10 @@
         def _():
             h_copy(f).start()
 
+        @pl.when(jnp.logical_and(f >= frames - 2, has_next))
+        def _():
+            g_copy(f + 2 - frames).wait_recv()
+
         grad_hidden = dot(three(g_ext, f, f + 1, f + 2), wtb[...])
         grad_pre = grad_hidden * sigma * (1.0 + pre * (1.0 - sigma))
         gp[f, pl.ds(1, rows)] = grad_pre.astype(BF16).reshape(rows, cols, ch)
@@ -247,7 +267,7 @@
         gi[f] = value.astype(BF16).reshape(rows, cols, ch)
         gi_copy(f).start()
 
-    pl.loop(frames - 2, frames)(grad_in)
+    pl.loop(0, 2)(grad_in)
 
     own = acc[pl.ds(pl.multiple_of(me_h * piece, piece), piece)]
     for step in range(1, n_h):
@@ -268,7 +288,7 @@
     for step in range(1, n_dp):
         dp_copy(step).start()
 
-    pl.loop(0, frames - 2)(grad_in)
+    pl.loop(2, frames)(grad_in)
 
     for step in range(1, n_dp):
         dp_from(step).wait_recv()
@@ -288,31 +308,38 @@
         at = res.at[pl.ds(pl.multiple_of(me_tm * chunk + src * piece, piece), piece)]
         return remote(at, at, ag1_s.at[step - 1], ag1_r.at[step - 1], "height", src)
 
+    far, near = lax.rem(me_tm + n_tm // 2, n_tm), me_tm + 1 - 2 * lax.rem(me_tm, 2)
+
+    def at_piece(tm, height):
+        return res.at[pl.ds(pl.multiple_of(tm * chunk + height * piece, piece), piece)]
+
+    def ag2_copy(tm, step, kind):
+        at = at_piece(tm, lax.rem(me_h + n_h - step, n_h))
+        return remote(
+            at, at, ag2_s.at[kind, step], ag2_r.at[kind, step], "tm", far if kind == 0 else near
+        )
+
     for step in range(1, n_h):
         ag1_copy(step).start()
-    for step in range(1, n_h):
-        ag1_from(step).wait_recv()
-
-    def ag2_copy(step):
-        peer = lax.rem(me_tm + step, n_tm)
-        at = res.at[pl.ds(pl.multiple_of(me_tm * chunk, chunk), chunk)]
-        return remote(at, at, ag2_s.at[step - 1], ag2_r.at[step - 1], "tm", peer)
-
-    def ag2_from(step):
-        src = lax.rem(me_tm + n_tm - step, n_tm)
-        at = res.at[pl.ds(pl.multiple_of(src * chunk, chunk), chunk)]
-        return remote(at, at, ag2_s.at[step - 1], ag2_r.at[step - 1], "tm", src)
-
-    for step in range(1, n_tm):
-        ag2_copy(step).start()
-    for step in range(1, n_tm):
-        ag2_from(step).wait_recv()
+    for step in range(n_h):
+        if step > 0:
+            ag1_from(step).wait_recv()
+        ag2_copy(me_tm, step, 0).start()
+        ag2_copy(me_tm, step, 1).start()
+    for step in range(n_h):
+        ag2_copy(far, step, 0).wait_recv()
+        ag2_copy(far, step, 2).start()
+    for step in range(n_h):
+        ag2_copy(near, step, 1).wait_recv()
+        ag2_copy(near, step, 2).wait_recv()
     res_out = pltpu.make_async_copy(res, res_hbm, loc.at[3 + frames])
     res_out.start()
 
-    pl.when(has_down)(x_down.wait_send)
-    pl.when(has_up)(x_up.wait_send)
-    pl.when(has_prev)(g_prev.wait_send)
+    for f in range(frames):
+        pl.when(has_down)(x_copy(f, 0).wait_send)
+        pl.when(has_up)(x_copy(f, 1).wait_send)
+    for f in range(2):
+        pl.when(has_prev)(g_copy(f).wait_send)
 
     @pl.when(has_next)
     def _():
@@ -324,7 +351,9 @@
         pl.when(has_up)(p_copy(f, 1).wait_send)
     for step in range(1, n_tm):
         rs1_copy(step)[1].wait_send()
-        ag2_copy(step).wait_send()
+    for step in range(n_h):
+        for kind in range(3):
+            ag2_copy(me_tm, step, kind).wait_send()
     for step in range(1, n_h):
         rs2_copy(step).wait_send()
         ag1_copy(step).wait_send()
@@ -339,12 +368,11 @@
 def per_device(sizes, frames_in, grad_out, w_spatial, w_temporal):
     clips, frames, rows, cols, ch = frames_in.shape
     n_dp, n_tm, n_h = sizes
-    assert clips == 1 and (12 * ch) % (n_tm * n_h) == 0
+    assert clips == 1 and n_tm == 4 and frames > 2 and (12 * ch) % (n_tm * n_h) == 0
     chunk = 12 * ch // n_tm
     piece = chunk // n_h
     factor = 1.0 / math.sqrt(clips * frames * rows * cols * n_dp * n_tm * n_h)
     any_spec = pl.BlockSpec(memory_space=pl.ANY)
-    vmem_spec = pl.BlockSpec(memory_space=pltpu.VMEM)
     dma = pltpu.SemaphoreType.DMA
     layer_out, grad_in, sums = pl.pallas_call(
         functools.partial(kernel, sizes, (frames, rows, cols, ch), factor),
@@ -353,9 +381,11 @@
             jax.ShapeDtypeStruct(frames_in.shape, BF16),
             jax.ShapeDtypeStruct((12 * ch, ch), BF16),
         ),
-        in_specs=[any_spec, any_spec, vmem_spec, vmem_spec],
+        in_specs=[any_spec] * 4,
         out_specs=(any_spec, any_spec, any_spec),
         scratch_shapes=[
+            pltpu.VMEM((3, 3, ch, ch), BF16),
+            pltpu.VMEM((3, ch, ch), BF16),
             pltpu.VMEM((frames, rows + 2, cols, ch), BF16),
             pltpu.VMEM((frames, rows + 2, cols, 3 * ch), BF16),
             pltpu.VMEM((frames + 2, rows, cols, ch), BF16),
@@ -373,15 +403,15 @@
             pltpu.VMEM((12 * ch, ch), BF16),
             pltpu.VMEM((frames, rows, cols, ch), BF16),
             pltpu.VMEM((frames, rows, cols, ch), BF16),
-            dma((4 + frames,)),
-            dma((2,)), dma((2,)), dma((1,)), dma((1,)),
+            dma((6 + frames,)),
+            dma((frames, 2)), dma((frames, 2)), dma((2,)), dma((2,)),
             dma((frames,)), dma((frames,)), dma((frames, 2)), dma((frames, 2)),
             dma((n_tm - 1,)), dma((n_tm - 1,)), dma((n_h - 1,)), dma((n_h - 1,)),
             dma((n_dp,)), dma((n_dp,)),
-            dma((n_h - 1,)), dma((n_h - 1,)), dma((n_tm - 1,)), dma((n_tm - 1,)),
+            dma((n_h - 1,)), dma((n_h - 1,)), dma((3, n_h)), dma((3, n_h)),
         ],
         compiler_params=pltpu.CompilerParams(
-            collective_id=0, has_side_effects=True, vmem_limit_bytes=48 << 20
+            collective_id=0, has_side_effects=True, vmem_limit_bytes=63 << 20
         ),
     )(frames_in, grad_out, w_spatial, w_temporal)
     sums = sums.astype(F32)

time: 50.4 us -> 44.2 us (0.88)
  Pallas kernels: 42.2 us -> 38.5 us
  local copies, waits for them, and re-layouts: 7.35 us -> 4.85 us
    pallas_call x1, Pallas kernels: 42.2 us -> 38.5 us  [per_device(): pl.pallas_call(functools.partial(kernel, sizes, (frames, rows, cols, ch),...]
    unnamed x10 -> x8, local copies, waits for them, and re-layouts: 5.8 us -> 2.25 us
    slice x1, local copies, waits for them, and re-layouts: 0.85 us -> 1.91 us  [per_device(): sums[:9 * ch].reshape(3, 3, ch, ch)]
where the time goes in v2:
time: 44.2 us; the launch traced here: 44 us
  Pallas kernels  38.5 us (87%)
  local copies, waits for them, and re-layouts  4.85 us (11%)
  between operations  0.66 us (1%)
    pallas_call x1, Pallas kernels, per_device(): pl.pallas_call(functools.partial(kernel, sizes, (frames, rows, cols, ch),...  38.5 us
    unnamed x8, local copies, waits for them, and re-layouts  2.25 us
    slice x1, local copies, waits for them, and re-layouts, per_device(): sums[:9 * ch].reshape(3, 3, ch, ch)  1.91 us

profile of v2, /device:TPU:1, one launch (start us, length us, event | category | flops | bytes accessed | tf_op | source)
XLA Modules:
  0.0 44.0 jit_solution(13891779056986851323)
XLA Ops:
  0.6 38.5 %shard_map.75 = (bf16[1,3,3,320,128]{4,3,2,1,0:T(8,128)(2,1)}, bf16[1,3,3,320,128]{4,3,2,1,0:T(8,128)(2,1)}, bf16[1536,128]{1,0:T(8,128)(2,1)}) custom-call(bf16[1,3,3,320,128]{4,3,2,1,0:T(8,128)(2,1)} %x_hbm.1, bf16[1,3,3,320,128]{4,3,2,1,0:T(8,128)(2,1)} %g_hbm.1, bf16[3,3,128,128]{3,2,1,0:T(8,128)(2,1)} %ws_hbm.1, bf16[3,128,128]{2,1,0:T(8,128)(2,1)} %wt_hbm.1), custom_call_target="tpu_custom_call" | custom-call | tf_op jit(solution)/shard_map/pallas_call | solution.py:377
  39.2 0.0 copy-start
  39.2 0.0 copy-start.2
  39.2 1.9 %slice.8 = f32[1152,128]{1,0:T(8,128)} slice(bf16[1536,128]{1,0:T(8,128)(2,1)} %get-tuple-element.9), slice={[0:1152], [0:128]} | slice | bytes 1179648 | tf_op jit(solution)/shard_map/slice | solution.py:421
  41.1 0.0 copy-done
  41.1 0.7 %slice.9 = f32[384,128]{1,0:T(8,128)} slice(bf16[1536,128]{1,0:T(8,128)(2,1)S(1)} %copy-done), slice={[1152:1536], [0:128]} | slice | bytes 393216 | tf_op jit(solution)/shard_map/slice | solution.py:422
  41.8 0.0 copy-done.2
  41.8 0.0 copy-start.1
  41.8 0.9 %copy.10 = bf16[1,3,3,320,128]{4,3,2,1,0:T(8,128)(2,1)} copy(bf16[1,3,3,320,128]{4,3,2,1,0:T(8,128)(2,1)S(1)} %copy-done.2) | data formatting | bytes 1474560
  42.7 0.5 %copy-done.1 = bf16[1,3,3,320,128]{4,3,2,1,0:T(8,128)(2,1)S(1)} copy-done((bf16[1,3,3,320,128]{4,3,2,1,0:T(8,128)(2,1)S(1)}, bf16[1,3,3,320,128]{4,3,2,1,0:T(8,128)(2,1)}, u32[]{:S(2)}) %copy-start.1) | copy-done | bytes 737304
  43.2 0.9 %copy.11 = bf16[1,3,3,320,128]{4,3,2,1,0:T(8,128)(2,1)} copy(bf16[1,3,3,320,128]{4,3,2,1,0:T(8,128)(2,1)S(1)} %copy-done.1) | data formatting | bytes 1474560
Async XLA Ops:
  39.2 1.9 %copy-start = (bf16[1536,128]{1,0:T(8,128)(2,1)S(1)}, bf16[1536,128]{1,0:T(8,128)(2,1)}, u32[]{:S(2)}) copy-start(bf16[1536,128]{1,0:T(8,128)(2,1)} %get-tuple-element.9) | copy-start | bytes 1179652
  39.2 2.6 %copy-start.2 = (bf16[1,3,3,320,128]{4,3,2,1,0:T(8,128)(2,1)S(1)}, bf16[1,3,3,320,128]{4,3,2,1,0:T(8,128)(2,1)}, u32[]{:S(2)}) copy-start(bf16[1,3,3,320,128]{4,3,2,1,0:T(8,128)(2,1)} %get-tuple-element.14) | copy-start | bytes 2211844
  41.8 1.4 %copy-start.1 = (bf16[1,3,3,320,128]{4,3,2,1,0:T(8,128)(2,1)S(1)}, bf16[1,3,3,320,128]{4,3,2,1,0:T(8,128)(2,1)}, u32[]{:S(2)}) copy-start(bf16[1,3,3,320,128]{4,3,2,1,0:T(8,128)(2,1)} %get-tuple-element.15) | copy-start | bytes 2211844

commit v3 on v2

--- a/solution.py
+++ b/solution.py
@@ -372,6 +372,10 @@
     chunk = 12 * ch // n_tm
     piece = chunk // n_h
     factor = 1.0 / math.sqrt(clips * frames * rows * cols * n_dp * n_tm * n_h)
+    operands = [
+        pltpu.with_memory_space_constraint(a, pltpu.HBM)
+        for a in (frames_in, grad_out, w_spatial, w_temporal)
+    ]
     any_spec = pl.BlockSpec(memory_space=pl.ANY)
     dma = pltpu.SemaphoreType.DMA
     layer_out, grad_in, sums = pl.pallas_call(
@@ -411,9 +415,9 @@
             dma((n_h - 1,)), dma((n_h - 1,)), dma((3, n_h)), dma((3, n_h)),
         ],
         compiler_params=pltpu.CompilerParams(
-            collective_id=0, has_side_effects=True, vmem_limit_bytes=63 << 20
+            collective_id=0, has_side_effects=True, vmem_limit_bytes=48 << 20
         ),
-    )(frames_in, grad_out, w_spatial, w_temporal)
+    )(*operands)
     sums = sums.astype(F32)
     return (
         layer_out,

time: 44.2 us -> 42.1 us (0.952)
  local copies, waits for them, and re-layouts: 4.85 us -> 3.27 us
    slice x1, local copies, waits for them, and re-layouts: 1.91 us -> 0.85 us  [per_device(): sums[:9 * ch].reshape(3, 3, ch, ch)]
    unnamed x8 -> x2, local copies, waits for them, and re-layouts: 2.25 us -> 1.73 us
    pallas_call x1, Pallas kernels: 38.5 us -> 38.1 us  [per_device(): pl.pallas_call(functools.partial(kernel, sizes, (frames, rows, cols, ch),...]
where the time goes in v3:
time: 42.1 us; the launch traced here: 42 us
  Pallas kernels  38.1 us (90%)
  local copies, waits for them, and re-layouts  3.27 us (8%)
  between operations  0.64 us (2%)
    pallas_call x1, Pallas kernels, per_device(): pl.pallas_call(functools.partial(kernel, sizes, (frames, rows, cols, ch),...  38.1 us
    unnamed x2, local copies, waits for them, and re-layouts  1.73 us
    slice x1, local copies, waits for them, and re-layouts, per_device(): sums[:9 * ch].reshape(3, 3, ch, ch)  0.85 us

profile of v3, /device:TPU:1, one launch (start us, length us, event | category | flops | bytes accessed | tf_op | source)
XLA Modules:
  0.0 42.0 jit_solution(13265914944446936995)
XLA Ops:
  0.6 38.1 %shard_map.75 = (bf16[1,3,3,320,128]{4,3,2,1,0:T(8,128)(2,1)S(1)}, bf16[1,3,3,320,128]{4,3,2,1,0:T(8,128)(2,1)S(1)}, bf16[1536,128]{1,0:T(8,128)(2,1)S(1)}) custom-call(bf16[1,3,3,320,128]{4,3,2,1,0:T(8,128)(2,1)} %x_hbm.1, bf16[1,3,3,320,128]{4,3,2,1,0:T(8,128)(2,1)} %g_hbm.1, bf16[3,3,128,128]{3,2,1,0:T(8,128)(2,1)} %ws_hbm.1, bf16[3,128,128]{2,1,0:T(8,128)(2,1)} %wt_hbm.1), custom_call_target="tpu_custom_call" | custom-call | tf_op jit(solution)/shard_map/pallas_call | solution.py:381
  38.7 0.9 %slice.8 = f32[1152,128]{1,0:T(8,128)} slice(bf16[1536,128]{1,0:T(8,128)(2,1)S(1)} %get-tuple-element.9), slice={[0:1152], [0:128]} | slice | bytes 1179648 | tf_op jit(solution)/shard_map/slice | solution.py:425
  39.6 0.7 %slice.9 = f32[384,128]{1,0:T(8,128)} slice(bf16[1536,128]{1,0:T(8,128)(2,1)S(1)} %get-tuple-element.9), slice={[1152:1536], [0:128]} | slice | bytes 393216 | tf_op jit(solution)/shard_map/slice | solution.py:426
  40.3 0.9 %copy.10 = bf16[1,3,3,320,128]{4,3,2,1,0:T(8,128)(2,1)} copy(bf16[1,3,3,320,128]{4,3,2,1,0:T(8,128)(2,1)S(1)} %get-tuple-element.14) | data formatting | bytes 1474560
  41.1 0.9 %copy.11 = bf16[1,3,3,320,128]{4,3,2,1,0:T(8,128)(2,1)} copy(bf16[1,3,3,320,128]{4,3,2,1,0:T(8,128)(2,1)S(1)} %get-tuple-element.15) | data formatting | bytes 1474560
